TPU v7x, 32 devices: a whole 2x2x4 slice. The times are simulated.
32 devices in a mesh: shot: 8 (over z, y), xline: 4 (over x, core).
Axes of the slice: x: 2, y: 2, z: 4, core: 2. Of those that a mesh axis runs over, the one named last changes fastest.
Arguments:
- records: bfloat16 [4, 16, 256, 2048], P('xline', 'shot'), may hold values from -1.796875 to 1.796875
- targets: bfloat16 [2048, 32, 256], P('xline', 'shot'), may hold values from -1.796875 to 1.796875
- aperture: int32 [32, 4, 16], P('shot', 'xline'), may hold values from 0 to 255
Outputs:
- multiples: bfloat16 [2048, 32, 256], P('xline', 'shot')
Inputs may be any that keep to these rules, and one draw needn't show every extreme that they name: An aperture entry is the receiver of the output shot at which the contributing source lies.
All inputs are finite; a program needn't handle non-finite values.
Results may differ from a plain program's by a relative error of at most 0.0071.
Values may be sent and summed in bfloat16 or wider, within the bound.
A program may use at most 128 MiB of HBM per device.

v0:
```python
import functools
import math

import jax
import jax.numpy as jnp
from jax import lax
from jax.experimental import pallas as pl
from jax.experimental.pallas import tpu as pltpu
from jax.sharding import PartitionSpec as P

NT = 2048
NF = 256
LOW = 32


def fourier_table(bins, start, count):
    blocks = NF // bins
    freq = jnp.arange(1, NF + 1, dtype=jnp.int32).reshape(blocks, 1, bins)
    freq = jnp.broadcast_to(freq, (blocks, 2, bins)).reshape(1, 2 * NF)
    is_imag = jnp.arange(2, dtype=jnp.int32).reshape(1, 2, 1)
    is_imag = jnp.broadcast_to(is_imag, (blocks, 2, bins)).reshape(1, 2 * NF) == 1

    def trig(times):
        angles = (times[:, None] * freq % NT).astype(jnp.float32) * (2.0 * math.pi / NT)
        return jnp.cos(angles), jnp.sin(angles)

    cos_hi, sin_hi = trig(start + jnp.arange(count // LOW, dtype=jnp.int32) * LOW)
    cos_lo, sin_lo = trig(jnp.arange(LOW, dtype=jnp.int32))
    scale = 1.0 / math.sqrt(NT)
    first = jnp.where(is_imag, -sin_hi, cos_hi) * scale
    second = jnp.where(is_imag, -cos_hi, -sin_hi) * scale
    first, second, cos_lo, sin_lo = lax.optimization_barrier((first, second, cos_lo, sin_lo))
    table = first[:, None] * cos_lo[None] + second[:, None] * sin_lo[None]
    return table.reshape(count, 2 * NF).astype(jnp.bfloat16)


def mix_kernel(lines, columns, held, bins, shots, spectra_ref, picked_ref, out_ref):
    gathers = columns * held
    receivers = out_ref.shape[1]
    rows = columns * bins
    depth = columns * 2 * bins
    taken = 2 * shots * gathers
    wide = held * depth

    k = lax.broadcasted_iota(jnp.int32, (taken, wide), 0)
    j = lax.broadcasted_iota(jnp.int32, (taken, wide), 1)
    k_imag, k_shot, k_gather = k // (shots * gathers), k // gathers % shots, k % gathers
    j_held, j_column, j_imag = j // depth, j % depth // (2 * bins), j // bins % 2
    same = k_gather == j_column * held + j_held
    crossed = k_imag != j_imag
    expand = []
    for shot in range(shots):
        for part in range(2):
            hit = same & (k_shot == shot) & (crossed if part else ~crossed)
            value = jnp.where(hit, 1.0, 0.0)
            if part == 0:
                value = jnp.where(j_imag == 1, -value, value)
            expand.append(value.astype(jnp.bfloat16))
    bin_of_row = lax.broadcasted_iota(jnp.int32, (rows, wide), 0) % bins
    bin_of_column = lax.broadcasted_iota(jnp.int32, (rows, wide), 1) % bins
    same_bin = bin_of_row == bin_of_column

    total = jnp.zeros(out_ref.shape, jnp.float32)
    for line in range(lines):
        block = picked_ref[line * rows : (line + 1) * rows, :]
        mixing = [
            jnp.where(
                same_bin, jnp.dot(block, matrix, preferred_element_type=jnp.float32), 0.0
            ).astype(jnp.bfloat16)
            for matrix in expand
        ]
        held_rows = slice(line * depth, (line + 1) * depth)
        spectra = jnp.concatenate(
            [spectra_ref[held_rows, h * receivers : (h + 1) * receivers] for h in range(held)], axis=0
        )
        total += jnp.dot(
            jnp.concatenate(mixing, axis=0), spectra, preferred_element_type=jnp.float32
        )
    out_ref[...] = total.astype(out_ref.dtype)


def spread_kernel(
    lines, columns, gathers, spectra_ref, targets_ref, aperture_ref, table_ref,
    spectra_out, picked_out,
    apertures, traces_here, traces, picked, send, recv, own, line_send, line_recv,
):
    devices = lines * columns
    line = lax.axis_index("xline")
    shot_here = lax.axis_index("shot")
    shots, time_rows, receivers = targets_ref.shape
    width = traces.shape[2]
    me = lax.axis_index("xline") * columns + lax.axis_index("shot")
    mesh_id = pl.DeviceIdType.MESH
    barrier = pltpu.get_barrier_semaphore()

    def greet(step, _):
        peer = lax.rem(me + step, devices)
        pl.semaphore_signal(
            barrier, inc=1,
            device_id={"xline": peer // columns, "shot": lax.rem(peer, columns)},
            device_id_type=mesh_id,
        )
        return 0

    lax.fori_loop(1, devices, greet, 0)
    pl.semaphore_wait(barrier, devices - 1)

    def line_of(step):
        far, other = step // columns // 2, lax.rem(step // columns, 2)
        moved = lax.rem(line + far * (lines // 2), lines)
        return moved + other * (1 - 2 * lax.rem(moved, 2))

    def copy_of(which, source, target, step):
        peer = line_of(step) * columns + lax.rem(shot_here + step, columns)
        return pltpu.make_async_remote_copy(
            src_ref=source.at[peer],
            dst_ref=target.at[me],
            send_sem=send.at[which, step],
            recv_sem=recv.at[which, step],
            device_id={"xline": peer // columns, "shot": lax.rem(peer, columns)},
            device_id_type=mesh_id,
        )

    def arrival_of(which, target, step):
        origin = line_of(step) * columns + lax.rem(shot_here + devices - step, columns)
        return pltpu.make_async_remote_copy(
            src_ref=target.at[origin],
            dst_ref=target.at[origin],
            send_sem=send.at[which, step],
            recv_sem=recv.at[which, step],
            device_id={"xline": origin // columns, "shot": lax.rem(origin, columns)},
            device_id_type=mesh_id,
        )

    def along_line(which, source, target, step):
        peer = lax.rem(line + step, lines)
        return pltpu.make_async_remote_copy(
            src_ref=source.at[peer] if which else source,
            dst_ref=target.at[line],
            send_sem=line_send.at[which, step],
            recv_sem=line_recv.at[which, step],
            device_id={"xline": peer},
            device_id_type=mesh_id,
        )

    def from_line(which, target, step):
        origin = lax.rem(line + lines - step, lines)
        return pltpu.make_async_remote_copy(
            src_ref=target.at[origin],
            dst_ref=target.at[origin],
            send_sem=line_send.at[which, step],
            recv_sem=line_recv.at[which, step],
            device_id={"xline": origin},
            device_id_type=mesh_id,
        )

    def begin(step, _):
        copy_of(0, spectra_ref, spectra_out, step).start()
        return 0

    for step in range(1, lines):
        along_line(0, aperture_ref, apertures, step).start()
    lax.fori_loop(1, 2 * columns, begin, 0)
    mine = [
        pltpu.make_async_copy(aperture_ref, apertures.at[line], own.at[0]),
        pltpu.make_async_copy(spectra_ref.at[me], spectra_out.at[me], own.at[1]),
    ]
    for copy in mine:
        copy.start()
    for copy in mine:
        copy.wait()
    for step in range(1, lines):
        from_line(0, apertures, step).wait_recv()

    wanted = []
    for l in range(lines):
        wanted += [apertures[l, s : s + 1, :] for s in range(shots)]
        if width > shots * gathers:
            wanted.append(jnp.zeros((1, width - shots * gathers), jnp.int32))
    wanted = jnp.concatenate(wanted, axis=1)
    lane = lax.broadcasted_iota(jnp.int32, (receivers, lines * width), 1)
    receiver = lax.broadcasted_iota(jnp.int32, (receivers, lines * width), 0)
    total = jnp.zeros((time_rows, lines * width), jnp.float32)
    for shot in range(shots):
        hit = (lane % width // gathers == shot) & (receiver == wanted)
        onehot = jnp.where(hit, 1.0, 0.0).astype(jnp.bfloat16)
        total += jnp.dot(targets_ref[shot], onehot, preferred_element_type=jnp.float32)
    total = total.astype(jnp.bfloat16)
    for l in range(lines):
        traces_here[l] = total[:, l * width : (l + 1) * width]

    arrival_of(0, spectra_out, 1).wait_recv()
    for step in range(1, lines):
        along_line(1, traces_here, traces, step).start()
    lax.fori_loop(2 * columns, devices, begin, 0)
    keep = pltpu.make_async_copy(traces_here.at[line], traces.at[line], own.at[2])
    keep.start()
    keep.wait()
    for step in range(1, lines):
        from_line(1, traces, step).wait_recv()

    value = jnp.zeros((table_ref.shape[1], width), jnp.float32)
    for l in range(lines):
        value += lax.dot_general(
            table_ref[l * time_rows : (l + 1) * time_rows, :], traces[l],
            (((0,), (0,)), ((), ())),
            preferred_element_type=jnp.float32,
        )
    picked[...] = value.astype(jnp.bfloat16).reshape(picked.shape)
    arrival_of(0, spectra_out, 2).wait_recv()

    def begin_picked(step, _):
        copy_of(1, picked, picked_out, step).start()
        return 0

    lax.fori_loop(1, devices, begin_picked, 0)
    keep = pltpu.make_async_copy(picked.at[me], picked_out.at[me], own.at[3])
    keep.start()
    keep.wait()
    for step in range(1, lines):
        along_line(0, aperture_ref, apertures, step).wait_send()
        along_line(1, traces_here, traces, step).wait_send()

    def finish(step, _):
        copy_of(0, spectra_ref, spectra_out, step).wait_send()
        copy_of(1, picked, picked_out, step).wait_send()
        arrival_of(1, picked_out, step).wait_recv()
        return 0

    def arrived(step, _):
        arrival_of(0, spectra_out, step).wait_recv()
        return 0

    lax.fori_loop(3, devices, arrived, 0)
    lax.fori_loop(1, devices, finish, 0)


def collect_kernel(lines, columns, running_ref, out_ref, send, recv, own):
    line = lax.axis_index("xline")
    me = lax.axis_index("shot")
    core_line = line + 1 - 2 * lax.rem(line, 2)
    far_line = lax.rem(line + lines // 2, lines)
    diagonal_line = lax.rem(core_line + lines // 2, lines)
    mesh_id = pl.DeviceIdType.MESH
    barrier = pltpu.get_barrier_semaphore()

    def greet(step, _):
        pl.semaphore_signal(
            barrier, inc=1, device_id={"shot": lax.rem(me + step, columns)}, device_id_type=mesh_id
        )
        return 0

    lax.fori_loop(1, columns, greet, 0)
    for peer in (core_line, far_line):
        pl.semaphore_signal(barrier, inc=1, device_id={"xline": peer}, device_id_type=mesh_id)
    pl.semaphore_wait(barrier, columns + 1)

    def across(step):
        peer = lax.rem(me + step, columns)
        return pltpu.make_async_remote_copy(
            src_ref=running_ref.at[peer],
            dst_ref=out_ref.at[line * columns + me],
            send_sem=send.at[0, step],
            recv_sem=recv.at[0, step],
            device_id={"shot": peer},
            device_id_type=mesh_id,
        )

    def onward(stage, source_line, peer_line, step):
        slot = source_line * columns + lax.rem(me + columns - step, columns)
        return pltpu.make_async_remote_copy(
            src_ref=out_ref.at[slot],
            dst_ref=out_ref.at[slot],
            send_sem=send.at[stage, step],
            recv_sem=recv.at[stage, step],
            device_id={"xline": peer_line},
            device_id_type=mesh_id,
        )

    def begin(step, _):
        across(step).start()
        return 0

    lax.fori_loop(1, columns, begin, 0)
    mine = pltpu.make_async_copy(running_ref.at[me], out_ref.at[line * columns + me], own.at[0])
    mine.start()
    mine.wait()
    onward(2, line, far_line, 0).start()
    onward(1, line, core_line, 0).start()

    def relay(step, _):
        slot = line * columns + lax.rem(me + columns - step, columns)
        pltpu.make_async_remote_copy(
            src_ref=out_ref.at[slot],
            dst_ref=out_ref.at[slot],
            send_sem=send.at[0, step],
            recv_sem=recv.at[0, step],
            device_id={"shot": lax.rem(me + columns - step, columns)},
            device_id_type=mesh_id,
        ).wait_recv()
        onward(2, line, far_line, step).start()
        onward(1, line, core_line, step).start()
        return 0

    lax.fori_loop(1, columns, relay, 0)

    def turn(step, _):
        onward(2, far_line, far_line, step).wait_recv()
        onward(3, far_line, core_line, step).start()
        return 0

    lax.fori_loop(0, columns, turn, 0)

    def finish(step, _):
        onward(1, core_line, core_line, step).wait_recv()
        onward(3, diagonal_line, core_line, step).wait_recv()
        onward(1, line, core_line, step).wait_send()
        onward(2, line, far_line, step).wait_send()
        onward(3, far_line, core_line, step).wait_send()
        return 0

    lax.fori_loop(0, columns, finish, 0)

    def sent(step, _):
        across(step).wait_send()
        return 0

    lax.fori_loop(1, columns, sent, 0)


def on_device(records, targets, aperture):
    f32, bf16 = jnp.float32, jnp.bfloat16
    lines = lax.axis_size("xline")
    columns = lax.axis_size("shot")
    devices = lines * columns
    bins = NF // devices
    time_rows, shots, receivers = targets.shape
    held = records.shape[1]
    gathers = aperture.shape[2]
    table = fourier_table(bins, 0, NT)
    chosen = shots * gathers
    padded = -(-chosen // 128) * 128

    spectra = jnp.einsum(
        "tp,kt->pk", table, records.reshape(held * receivers, NT), preferred_element_type=f32
    ).astype(bf16)

    spectra = spectra.reshape(devices, 2 * bins, held * receivers)
    in_vmem = pl.BlockSpec(memory_space=pltpu.VMEM)
    dma = pltpu.SemaphoreType.DMA
    spectra, picked = pl.pallas_call(
        functools.partial(spread_kernel, lines, columns, gathers),
        out_shape=[
            jax.ShapeDtypeStruct(spectra.shape, bf16),
            jax.ShapeDtypeStruct((devices, 2 * bins, padded), bf16),
        ],
        in_specs=[in_vmem] * 4,
        out_specs=[in_vmem] * 2,
        scratch_shapes=[
            pltpu.VMEM((lines, shots, gathers), jnp.int32),
            pltpu.VMEM((lines, time_rows, padded), bf16),
            pltpu.VMEM((lines, time_rows, padded), bf16),
            pltpu.VMEM((devices, 2 * bins, padded), bf16),
            dma((2, devices)), dma((2, devices)), dma((4,)), dma((2, lines)), dma((2, lines)),
        ],
        compiler_params=pltpu.CompilerParams(collective_id=0, has_side_effects=True),
    )(spectra, targets.transpose(1, 0, 2), aperture.reshape(shots, gathers), table)
    picked = picked.reshape(devices, 2, bins, padded)[..., :chosen]
    picked = jnp.concatenate([picked[:, 0], picked[:, 1]], axis=-1)

    running = pl.pallas_call(
        functools.partial(mix_kernel, lines, columns, held, bins, shots),
        out_shape=jax.ShapeDtypeStruct((shots * 2 * columns * bins, receivers), bf16),
        in_specs=[pl.BlockSpec(memory_space=pltpu.VMEM)] * 2,
        out_specs=pl.BlockSpec(memory_space=pltpu.VMEM),
    )(spectra.reshape(2 * NF, held * receivers), picked.reshape(NF, -1))
    running = running.reshape(shots, 2, columns, bins, receivers).transpose(2, 0, 1, 3, 4)
    running = running.reshape(columns, shots, 2 * bins, receivers)
    running = pl.pallas_call(
        functools.partial(collect_kernel, lines, columns),
        out_shape=jax.ShapeDtypeStruct((devices, *running.shape[1:]), bf16),
        in_specs=[in_vmem],
        out_specs=in_vmem,
        scratch_shapes=[dma((4, columns)), dma((4, columns)), dma((1,))],
        compiler_params=pltpu.CompilerParams(collective_id=1, has_side_effects=True),
    )(running)
    running = running.transpose(0, 2, 1, 3).reshape(2 * NF, shots, receivers)

    rows = fourier_table(bins, lax.axis_index("xline") * time_rows, time_rows)
    out = jnp.einsum("tp,psr->tsr", rows * 2, running, preferred_element_type=f32)
    return out.astype(bf16)


def solution(mesh):
    in_specs = (P("xline", "shot", None, None), P("xline", "shot", None), P("shot", "xline", None))
    out_specs = P("xline", "shot", None)
    return jax.shard_map(
        on_device, mesh=mesh, in_specs=in_specs, out_specs=out_specs, check_vma=False
    )
```

profile of v0, /device:TPU:0, one launch (start us, length us, event | category | flops | bytes accessed | tf_op | source)
XLA Modules:
  0.0 64.0 jit_solution(961525669321689826)
XLA Ops:
  0.0 0.0 copy-start
  0.0 0.1 mul.246
  0.2 0.1 eq.32
  0.3 0.6 select_multiply_fusion
  0.9 0.3 fusion.14
  1.2 0.7 %add_convert_fusion = bf16[64,32,512]{2,1,0:T(8,128)(2,1)S(1)} fusion(f32[32,512]{1,0:T(8,128)S(1)} %get-tuple-element.22, f32[64,512]{1,0:T(8,128)S(1)} %get-tuple-element.21, f32[32,512]{1,0:T(8,128)S(1)} %get-tuple-element.20, f32[64,512]{1,0:T(8,128)S(1)} %get-tuple-element.19), kind=kLoop, calls=%fused_computation | loop fusion | flops 4194304 | bytes 2490368 | tf_op jit(solution)/shard_map/convert_element_type | solution.py:34
  1.9 0.0 copy-start.1
  1.9 0.0 copy-done
  1.9 0.0 copy-start.2
  1.9 2.1 %convolution_convert_fusion.1 = bf16[512,512]{1,0:T(8,128)(2,1)} fusion(bf16[2048,512]{1,0:T(8,128)(2,1)S(1)} %bitcast.33, bf16[512,2048]{1,0:T(8,128)(2,1)S(1)} %bitcast.32), kind=kOutput, calls=%fused_computation.2 | convolution fusion | flops 1074003968 | bytes 4718592 | tf_op jit(solution)/shard_map/tp,kt->pk/dot_general | solution.py:344
  4.0 0.0 copy-done.1
  4.0 0.0 copy-done.2
  4.0 1.1 %copy.19 = bf16[512,4,256]{2,0,1:T(8,128)(2,1)} copy(bf16[512,4,256]{2,1,0:T(4,128)(2,1)S(1)} %copy-done.2) | data formatting | bytes 2097152 | tf_op args[1]
  5.2 31.8 %shard_map.37 = (bf16[32,16,512]{2,1,0:T(8,128)(2,1)}, bf16[32,16,128]{2,1,0:T(8,128)(2,1)}) custom-call(bf16[32,16,512]{2,1,0:T(8,128)(2,1)} %bitcast.40, bf16[4,512,256]{2,1,0:T(8,128)(2,1)} %bitcast.35, s32[4,16]{1,0:T(4,128)} %bitcast.44, bf16[2048,512]{1,0:T(8,128)(2,1)} %bitcast.34), custom_call_target="tpu_custom_call" | custom-call | tf_op jit(solution)/shard_map/pallas_call | solution.py:351
  37.0 0.9 %slice_bitcast_fusion.1 = (bf16[256,64]{1,0:T(8,128)(2,1)S(1)}, bf16[256,64]{1,0:T(8,128)(2,1)S(1)}) fusion(bf16[32,2,8,128]{3,2,1,0:T(8,128)(2,1)} %bitcast.43), kind=kLoop, calls=%fused_computation.25 | loop fusion | bytes 131072 | tf_op jit(solution)/shard_map/concatenate | solution.py:369
  37.9 0.7 %pad_maximum_fusion.picked_ref = bf16[256,128]{1,0:T(8,128)(2,1)} fusion(bf16[256,64]{1,0:T(8,128)(2,1)S(1)} %get-tuple-element.26, bf16[256,64]{1,0:T(8,128)(2,1)S(1)} %get-tuple-element.25), kind=kLoop, calls=%fused_computation.26 | loop fusion | flops 131072 | bytes 131072 | tf_op jit(solution)/shard_map/concatenate | solution.py:369
  38.6 2.6 %shard_map.38 = bf16[512,256]{1,0:T(8,128)(2,1)} custom-call(bf16[512,512]{1,0:T(8,128)(2,1)} %bitcast.42, bf16[256,128]{1,0:T(8,128)(2,1)} %pad_maximum_fusion.picked_ref), custom_call_target="tpu_custom_call" | custom-call | tf_op jit(solution)/shard_map/pallas_call | solution.py:371
  41.3 1.7 %copy.20 = bf16[4,2,8,8,256]{4,3,1,0,2:T(8,128)(2,1)} copy(bf16[4,2,8,8,256]{4,3,2,1,0:T(8,128)(2,1)} %bitcast.39) | data formatting | bytes 524288 | tf_op jit(solution)/shard_map/reshape | solution.py:377
  42.9 16.9 %shard_map.39 = bf16[32,4,16,256]{3,2,1,0:T(8,128)(2,1)} custom-call(bf16[8,4,16,256]{3,2,1,0:T(8,128)(2,1)} %bitcast.37), custom_call_target="tpu_custom_call" | custom-call | tf_op jit(solution)/shard_map/pallas_call | solution.py:379
  59.8 1.3 %copy.13 = bf16[32,16,4,256]{3,1,0,2:T(8,128)(2,1)S(1)} copy(bf16[32,16,4,256]{3,1,2,0:T(8,128)(2,1)} %bitcast.36) | data formatting | bytes 2097152 | tf_op jit(solution)/shard_map/transpose | solution.py:387
  61.1 0.2 select_multiply_fusion.2
  61.4 0.2 fusion
  61.5 0.7 %convolution_convert_fusion = bf16[512,4,256]{2,0,1:T(8,128)(2,1)S(1)} fusion(bf16[512,512,1]{1,0,2:T(8,128)(2,1)S(1)} %bitcast.41, bf16[512,4,256]{2,0,1:T(8,128)(2,1)S(1)} %bitcast.38), kind=kOutput, calls=%fused_computation.1 | convolution fusion | flops 537395200 | bytes 2621440 | tf_op jit(solution)/shard_map/tp,psr->tsr/dot_general | solution.py:390
  62.3 1.8 %copy.14 = bf16[512,4,256]{2,1,0:T(4,128)(2,1)} copy(bf16[512,4,256]{2,0,1:T(8,128)(2,1)S(1)} %convolution_convert_fusion) | data formatting | bytes 2097152 | tf_op jit(solution)/shard_map/convert_element_type | solution.py:391
  (5 shorter events, 0.0 us)
Async XLA Ops:
  0.0 1.9 %copy-start = (bf16[1,2,256,2048]{3,2,1,0:T(8,128)(2,1)S(1)}, bf16[1,2,256,2048]{3,2,1,0:T(8,128)(2,1)}, u32[]{:S(2)}) copy-start(bf16[1,2,256,2048]{3,2,1,0:T(8,128)(2,1)} %param.3) | copy-start | bytes 6291460
  1.9 2.1 %copy-start.1 = (bf16[64,32,512]{2,1,0:T(8,128)(2,1)}, bf16[64,32,512]{2,1,0:T(8,128)(2,1)S(1)}, u32[]{:S(2)}) copy-start(bf16[64,32,512]{2,1,0:T(8,128)(2,1)S(1)} %add_convert_fusion) | copy-start | bytes 6291460
  1.9 2.1 %copy-start.2 = (bf16[512,4,256]{2,1,0:T(4,128)(2,1)S(1)}, bf16[512,4,256]{2,1,0:T(4,128)(2,1)}, u32[]{:S(2)}) copy-start(bf16[512,4,256]{2,1,0:T(4,128)(2,1)} %param.4) | copy-start | bytes 3145732
where the time goes:
time: 64.3 us; the launch traced here: 64 us
  Pallas kernels  51.4 us (80%)
  local copies, waits for them, and re-layouts  6.99 us (11%)
  matrix products  2.82 us (4%)
  other arithmetic  2.75 us (4%)
    pallas_call x1, Pallas kernels, on_device(): pl.pallas_call(functools.partial(spread_kernel, lines, columns, gathers),...  31.8 us
    pallas_call x1, Pallas kernels, on_device(): pl.pallas_call(functools.partial(collect_kernel, lines, columns), out_sha...  16.9 us
    pallas_call x1, Pallas kernels, on_device(): pl.pallas_call(functools.partial(mix_kernel, lines, columns, held, bins,...  2.64 us
    dot_general x1, matrix products, on_device(): jnp.einsum('tp,kt->pk', table, records.reshape(held * receivers, NT), pre...  2.1 us
    convert_element_type x1, local copies, waits for them, and re-layouts, on_device(): return out.astype(bf16)  1.78 us
    reshape x1, local copies, waits for them, and re-layouts, on_device(): running.reshape(shots, 2, columns, bins, receivers).transpose(2, 0, 1, 3, 4)  1.67 us
    transpose x1, local copies, waits for them, and re-layouts, on_device(): running = running.transpose(0, 2, 1, 3).reshape(2 * NF, shots, receivers)  1.31 us

commit v1 on v0

--- a/solution.py
+++ b/solution.py
@@ -328,6 +328,393 @@
     lax.fori_loop(1, columns, sent, 0)
 
 
+def xor_of(index, step):
+    result, weight = 0, 1
+    while weight < 64:
+        bit = lax.rem(index // weight + step // weight, 2)
+        result, weight = result + bit * weight, weight * 2
+    return result
+
+
+def fused_kernel(
+    lines, columns, bins, low,
+    records_ref, targets_ref, aperture_ref, out_ref,
+    records, table, inverse, expand, mixing, apertures, traces_here, traces,
+    sent, spectra, picked_here, picked, running, gathered,
+    load, own, near_send, near_recv, wide_send, wide_recv, run_send, run_recv,
+):
+    f32, bf16 = jnp.float32, jnp.bfloat16
+    devices = lines * columns
+    halves = records.shape[0]
+    shots, time_rows, receivers = targets_ref.shape
+    held = records_ref.shape[0] // receivers
+    part = receivers // halves
+    gathers = aperture_ref.shape[1]
+    chosen = shots * gathers
+    width = 2 * chosen
+    rows = columns * bins
+    depth = 2 * bins
+    line = lax.axis_index("xline")
+    shot_here = lax.axis_index("shot")
+    me = line * columns + shot_here
+    mesh_id = pl.DeviceIdType.MESH
+    barrier = pltpu.get_barrier_semaphore()
+
+    def greet(step, _):
+        peer = lax.rem(me + step, devices)
+        pl.semaphore_signal(
+            barrier, inc=1,
+            device_id={"xline": peer // columns, "shot": lax.rem(peer, columns)},
+            device_id_type=mesh_id,
+        )
+        return 0
+
+    lax.fori_loop(1, devices, greet, 0)
+
+    loads = []
+    for h in range(halves):
+        for g in range(held):
+            loads.append(
+                pltpu.make_async_copy(
+                    records_ref.at[pl.ds(g * receivers + h * part, part), :],
+                    records.at[h, pl.ds(g * part, part), :],
+                    load.at[h, g],
+                )
+            )
+    for copy in loads:
+        copy.start()
+
+    group = 4 * depth // 2
+    scale = 1.0 / math.sqrt(NT)
+    step_angle = 2.0 * math.pi / NT
+    row = lax.broadcasted_iota(jnp.int32, (group, 128), 0)
+    lane = lax.broadcasted_iota(jnp.int32, (group, 128), 1)
+    freq = row // depth * bins + row % bins + 1
+    turn = (row // bins % 2) * (NT // 4)
+    group_bins = group // depth * bins
+
+    def wave(first_freq, first_time):
+        angle = ((freq + first_freq) * (lane + first_time) + turn) % NT
+        return jnp.cos(angle.astype(f32) * step_angle) * scale
+
+    across_time = 2.0 * jnp.cos((freq * 128 % NT).astype(f32) * step_angle)
+    across_rows = 2.0 * jnp.cos((lane * group_bins % NT).astype(f32) * step_angle)
+    flip = (1 - 2 * (freq % 2)).astype(f32)
+
+    def fill(block, carry):
+        at0, next0, at1, next1 = carry
+        here = pl.ds(pl.multiple_of(block * group, group), group)
+        now, later = at0, at1
+        for k in range(NT // 256):
+            table[here, k * 128 : (k + 1) * 128] = now.astype(bf16)
+            table[here, NT // 2 + k * 128 : NT // 2 + (k + 1) * 128] = (now * flip).astype(bf16)
+            now, later = later, across_time * later - now
+        return next0, across_rows * next0 - at0, next1, across_rows * next1 - at1
+
+    lax.fori_loop(
+        0, 2 * NF // group, fill,
+        (wave(0, 0), wave(group_bins, 0), wave(0, 128), wave(group_bins, 128)),
+    )
+
+    def transform(h):
+        for g in range(held):
+            loads[h * held + g].wait()
+        value = lax.dot_general(
+            table[...], records[h], (((1,), (1,)), ((), ())), preferred_element_type=f32
+        )
+        sent[h] = value.astype(bf16).reshape(sent.shape[1:])
+
+    def wide(which, source, target, step):
+        far, near = step // 8, lax.rem(step, 8)
+        line_step = near // 4 * 2 + lax.rem(near, 2)
+        shot_step = far * 2 + lax.rem(near // 2, 2)
+        peer_line, peer_shot = xor_of(line, line_step), xor_of(shot_here, shot_step)
+        return pltpu.make_async_remote_copy(
+            src_ref=source.at[peer_line * columns + peer_shot],
+            dst_ref=target.at[me],
+            send_sem=wide_send.at[which, step],
+            recv_sem=wide_recv.at[which, step],
+            device_id={"xline": peer_line, "shot": peer_shot},
+            device_id_type=mesh_id,
+        )
+
+    def wide_copy(which, step):
+        if which < halves:
+            return wide(which, sent.at[which], spectra.at[which], step)
+        return wide(which, picked_here, picked, step)
+
+    def start_wide(which, first, last):
+        def begin(j, _):
+            wide_copy(which, devices - 1 - j).start()
+            return 0
+
+        lax.fori_loop(first, last, begin, 0)
+
+    def wait_wide(which):
+        def finish(j, _):
+            wide_copy(which, devices - 1 - j).wait()
+            return 0
+
+        lax.fori_loop(0, devices - 1, finish, 0)
+
+    def along_line(which, step):
+        peer = xor_of(line, step)
+        source = traces_here.at[peer] if which else aperture_ref
+        target = traces if which else apertures
+        return pltpu.make_async_remote_copy(
+            src_ref=source,
+            dst_ref=target.at[line],
+            send_sem=near_send.at[which, step],
+            recv_sem=near_recv.at[which, step],
+            device_id={"xline": peer},
+            device_id_type=mesh_id,
+        )
+
+    transform(0)
+    pl.semaphore_wait(barrier, devices - 1)
+    for step in range(1, lines):
+        along_line(0, step).start()
+    start_wide(0, 0, devices - 1)
+    mine = [
+        pltpu.make_async_copy(aperture_ref, apertures.at[line], own.at[0]),
+        pltpu.make_async_copy(sent.at[0, me], spectra.at[0, me], own.at[1]),
+    ]
+    for copy in mine:
+        copy.start()
+    transform(1)
+    keep_one = pltpu.make_async_copy(sent.at[1, me], spectra.at[1, me], own.at[2])
+    keep_one.start()
+    for copy in mine:
+        copy.wait()
+    for step in range(1, lines):
+        along_line(0, step).wait()
+
+    wanted = []
+    for l in range(lines):
+        wanted += [apertures[l, s : s + 1, :] for s in range(shots)] * 2
+    wanted = jnp.concatenate(wanted, axis=1)
+    lane = lax.broadcasted_iota(jnp.int32, (receivers, lines * width), 1)
+    receiver = lax.broadcasted_iota(jnp.int32, (receivers, lines * width), 0)
+    total = jnp.zeros((time_rows, lines * width), f32)
+    for shot in range(shots):
+        hit = (lane % chosen // gathers == shot) & (receiver == wanted)
+        onehot = jnp.where(hit, 1.0, 0.0).astype(bf16)
+        total += jnp.dot(targets_ref[shot], onehot, preferred_element_type=f32)
+    fold = time_rows // 2
+    lane = lax.broadcasted_iota(jnp.int32, (fold, lines * width), 1)
+    folded = jnp.where(lane % width < chosen, total[:fold], total[fold:]).astype(bf16)
+    for l in range(lines):
+        traces_here[l] = folded[:, l * width : (l + 1) * width]
+    for step in range(1, lines):
+        along_line(1, step).start()
+    keep = pltpu.make_async_copy(traces_here.at[line], traces.at[line], own.at[3])
+    keep.start()
+    start_wide(1, 0, low)
+
+    taken = width
+    across = held * columns * depth
+    for shot in range(shots):
+        for q in range(2):
+            k = lax.broadcasted_iota(jnp.int32, (taken, held * columns * depth), 0)
+            j = lax.broadcasted_iota(jnp.int32, (taken, held * columns * depth), 1)
+            k_imag, k_shot, k_gather = k // chosen, k // gathers % shots, k % gathers
+            j_held, j_column, j_imag = j // (columns * depth), j // depth % columns, j // bins % 2
+            hit = (k_gather == j_column * held + j_held) & (k_shot == shot)
+            hit = hit & ((k_imag != j_imag) if q else (k_imag == j_imag))
+            value = jnp.where(hit, 1.0, 0.0)
+            if q == 0:
+                value = jnp.where(j_imag == 1, -value, value)
+            expand[shot * 2 + q] = value.astype(bf16)
+    slab = line * time_rows
+    for c in range(time_rows // 128):
+        block = table[:, pl.ds(pl.multiple_of(slab + c * 128, 128), 128)].astype(f32)
+        inverse[c * 128 : (c + 1) * 128, :] = (block * 2.0).T.astype(bf16)
+
+    keep.wait()
+    for step in range(1, lines):
+        along_line(1, step).wait()
+    ahead = jnp.zeros((2 * NF, width), f32)
+    behind = jnp.zeros((2 * NF, width), f32)
+    for l in range(lines):
+        base = l * time_rows
+        ahead += jnp.dot(table[:, base : base + fold], traces[l], preferred_element_type=f32)
+        behind += jnp.dot(
+            table[:, base + fold : base + time_rows], traces[l], preferred_element_type=f32
+        )
+    real = (ahead + pltpu.roll(behind, chosen, 1)).reshape(devices, depth, width)[:, :bins]
+    imag = (pltpu.roll(ahead, chosen, 1) + behind).reshape(devices, depth, width)[:, bins:]
+    lane = lax.broadcasted_iota(jnp.int32, (devices, bins, width), 2)
+    picked_here[...] = jnp.where(lane < chosen, real, imag).astype(bf16)
+    start_wide(2, 0, devices - 1)
+    start_wide(1, low, devices - 1)
+    keep = pltpu.make_async_copy(picked_here.at[me], picked.at[me], own.at[4])
+    keep.start()
+
+    wait_wide(0)
+    keep.wait()
+    wait_wide(2)
+
+    same_bin = (
+        lax.broadcasted_iota(jnp.int32, (rows, across), 0) % bins
+        == lax.broadcasted_iota(jnp.int32, (rows, across), 1) % bins
+    )
+    span = columns * depth
+    for l in range(lines):
+        block = picked[l * columns : (l + 1) * columns].astype(f32).reshape(rows, width).astype(bf16)
+        for sq in range(2 * shots):
+            value = jnp.dot(block, expand[sq], preferred_element_type=f32)
+            value = jnp.where(same_bin, value, 0.0).astype(bf16)
+            for g in range(held):
+                first = (g * lines + l) * span
+                mixing[sq * rows : (sq + 1) * rows, first : first + span] = (
+                    value[:, g * span : (g + 1) * span]
+                )
+
+    def hop(h, stage, source_line, peer_line, step):
+        slot = source_line * columns + xor_of(shot_here, step)
+        return pltpu.make_async_remote_copy(
+            src_ref=gathered.at[h, slot],
+            dst_ref=gathered.at[h, slot],
+            send_sem=run_send.at[h, stage, step],
+            recv_sem=run_recv.at[h, stage, step],
+            device_id={"xline": peer_line},
+            device_id_type=mesh_id,
+        )
+
+    def spread(h, step):
+        peer = xor_of(shot_here, step)
+        return pltpu.make_async_remote_copy(
+            src_ref=running.at[h, peer],
+            dst_ref=gathered.at[h, me],
+            send_sem=run_send.at[h, 0, step],
+            recv_sem=run_recv.at[h, 0, step],
+            device_id={"shot": peer},
+            device_id_type=mesh_id,
+        )
+
+    core_line = xor_of(line, 1)
+    far_line = xor_of(line, 2)
+    diagonal_line = xor_of(line, 3)
+
+    def mix(h):
+        total = jnp.zeros((2 * shots * rows, part), f32)
+        for g in range(held):
+            block = spectra[h, :, :, g * part : (g + 1) * part].reshape(2 * NF, part)
+            total += jnp.dot(
+                mixing[:, g * 2 * NF : (g + 1) * 2 * NF], block, preferred_element_type=f32
+            )
+        for column in range(columns):
+            for shot in range(shots):
+                pieces = [
+                    total[(shot * 2 + q) * rows + column * bins :][:bins] for q in range(2)
+                ]
+                running[h, column, shot] = jnp.concatenate(pieces, axis=0).astype(bf16)
+
+        def begin(j, _):
+            spread(h, columns - 1 - j).start()
+            return 0
+
+        lax.fori_loop(0, columns - 1, begin, 0)
+        keep = pltpu.make_async_copy(running.at[h, shot_here], gathered.at[h, me], own.at[5 + h])
+        keep.start()
+        keep.wait()
+        hop(h, 2, line, far_line, 0).start()
+        hop(h, 1, line, core_line, 0).start()
+
+    def relay(h):
+        def pass_on(j, _):
+            step = j + 1
+            spread(h, step).wait()
+            hop(h, 2, line, far_line, step).start()
+            hop(h, 1, line, core_line, step).start()
+            return 0
+
+        lax.fori_loop(0, columns - 1, pass_on, 0)
+
+    def turn_over(h):
+        def pass_on(step, _):
+            hop(h, 2, far_line, far_line, step).wait_recv()
+            hop(h, 3, far_line, core_line, step).start()
+            return 0
+
+        lax.fori_loop(0, columns, pass_on, 0)
+
+    def complete(h):
+        def finish(step, _):
+            hop(h, 1, core_line, core_line, step).wait_recv()
+            hop(h, 3, diagonal_line, core_line, step).wait_recv()
+            hop(h, 1, line, core_line, step).wait_send()
+            hop(h, 2, line, far_line, step).wait_send()
+            hop(h, 3, far_line, core_line, step).wait_send()
+            return 0
+
+        lax.fori_loop(0, columns, finish, 0)
+
+    def invert(h):
+        for shot in range(shots):
+            block = gathered[h, :, shot].reshape(2 * NF, part)
+            out_ref[shot, :, h * part : (h + 1) * part] = jnp.dot(
+                inverse[...], block, preferred_element_type=f32
+            ).astype(bf16)
+
+    mix(0)
+    keep_one.wait()
+    wait_wide(1)
+    mix(1)
+    relay(0)
+    turn_over(0)
+    relay(1)
+    complete(0)
+    invert(0)
+    turn_over(1)
+    complete(1)
+    invert(1)
+
+
+def fused(records, targets, aperture):
+    bf16 = jnp.bfloat16
+    lines = lax.axis_size("xline")
+    columns = lax.axis_size("shot")
+    devices = lines * columns
+    bins = NF // devices
+    time_rows, shots, receivers = targets.shape
+    held = records.shape[1]
+    gathers = aperture.shape[2]
+    halves, part = 2, receivers // 2
+    width = 2 * shots * gathers
+    wide = held * columns * 2 * bins
+    in_vmem = pl.BlockSpec(memory_space=pltpu.VMEM)
+    dma = pltpu.SemaphoreType.DMA
+    vmem = lambda *shape: pltpu.VMEM(shape, bf16)
+    out = pl.pallas_call(
+        functools.partial(fused_kernel, lines, columns, bins, 10),
+        out_shape=jax.ShapeDtypeStruct((shots, time_rows, receivers), bf16),
+        in_specs=[pl.BlockSpec(memory_space=pl.ANY), in_vmem, in_vmem],
+        out_specs=in_vmem,
+        scratch_shapes=[
+            vmem(halves, held * part, NT),
+            vmem(2 * NF, NT),
+            vmem(time_rows, 2 * NF),
+            vmem(2 * shots, width, wide),
+            vmem(2 * shots * columns * bins, lines * wide),
+            pltpu.VMEM((lines, shots, gathers), jnp.int32),
+            vmem(lines, time_rows // 2, width),
+            vmem(lines, time_rows // 2, width),
+            vmem(halves, devices, 2 * bins, held * part),
+            vmem(halves, devices, 2 * bins, held * part),
+            vmem(devices, bins, width),
+            vmem(devices, bins, width),
+            vmem(halves, columns, shots, 2 * bins, part),
+            vmem(halves, devices, shots, 2 * bins, part),
+            dma((halves, held)), dma((7,)), dma((2, lines)), dma((2, lines)),
+            dma((3, devices)), dma((3, devices)),
+            dma((halves, 4, columns)), dma((halves, 4, columns)),
+        ],
+        compiler_params=pltpu.CompilerParams(collective_id=2, has_side_effects=True),
+    )(records.reshape(held * receivers, NT), targets.transpose(1, 0, 2), aperture.reshape(shots, gathers))
+    return out.transpose(1, 0, 2)
+
+
 def on_device(records, targets, aperture):
     f32, bf16 = jnp.float32, jnp.bfloat16
     lines = lax.axis_size("xline")
@@ -337,6 +724,8 @@
     time_rows, shots, receivers = targets.shape
     held = records.shape[1]
     gathers = aperture.shape[2]
+    if (lines, columns, bins, 2 * shots * gathers, receivers) == (4, 8, 8, 128, 256):
+        return fused(records, targets, aperture)
     table = fourier_table(bins, 0, NT)
     chosen = shots * gathers
     padded = -(-chosen // 128) * 128

time: 64.3 us -> 49.4 us (0.77)
  Pallas kernels: 51.4 us -> 43.8 us
  matrix products: 2.82 us -> 0 us
  other arithmetic: 2.75 us -> 0 us
  local copies, waits for them, and re-layouts: 6.99 us -> 5.34 us
    pallas_call x3 -> x1, Pallas kernels: 51.4 us -> 43.8 us  [fused(): pl.pallas_call(functools.partial(fused_kernel, lines, columns, bins, 10),...]
    dot_general x2 -> x0, matrix products: 2.82 us -> none  [the longest x1 2.1 us: on_device(): jnp.einsum('tp,kt->pk', table, records.reshape(held * receivers, NT), pre...]
    convert_element_type x1 -> x0, local copies, waits for them, and re-layouts: 1.78 us -> none  [on_device(): return out.astype(bf16)]
    transpose x1, local copies, waits for them, and re-layouts: 1.31 us -> 3.01 us  [fused(): return out.transpose(1, 0, 2)]
    reshape x1 -> x0, local copies, waits for them, and re-layouts: 1.67 us -> none  [on_device(): running.reshape(shots, 2, columns, bins, receivers).transpose(2, 0, 1, 3, 4)]
    unnamed x7 -> x1, local copies, waits for them, and re-layouts: 1.12 us -> 2.33 us
    mul x4 -> x0, other arithmetic: 1 us -> none  [the longest x2 0.84 us: fourier_table(): second = jnp.where(is_imag, -cos_hi, -sin_hi) * scale]
    concatenate x1 -> x0, local copies, waits for them, and re-layouts: 0.88 us -> none  [on_device(): picked = jnp.concatenate([picked[:, 0], picked[:, 1]], axis=-1)]
where the time goes in v1:
time: 49.4 us; the launch traced here: 49.1 us
  Pallas kernels  43.8 us (89%)
  local copies, waits for them, and re-layouts  5.34 us (11%)
    pallas_call x1, Pallas kernels, fused(): pl.pallas_call(functools.partial(fused_kernel, lines, columns, bins, 10),...  43.8 us
    transpose x1, local copies, waits for them, and re-layouts, fused(): return out.transpose(1, 0, 2)  3.01 us
    unnamed x1, local copies, waits for them, and re-layouts  2.33 us

profile of v1, /device:TPU:0, one launch (start us, length us, event | category | flops | bytes accessed | tf_op | source)
XLA Modules:
  0.0 49.1 jit_solution(10385877586456958592)
XLA Ops:
  0.0 2.3 %copy.7 = bf16[512,4,256]{2,0,1:T(8,128)(2,1)} copy(bf16[512,4,256]{2,1,0:T(4,128)(2,1)} %param.4) | data formatting | bytes 2097152 | tf_op args[1]
  2.3 43.8 %shard_map.37 = bf16[4,512,256]{2,1,0:T(8,128)(2,1)} custom-call(bf16[512,2048]{1,0:T(8,128)(2,1)} %bitcast.8, bf16[4,512,256]{2,1,0:T(8,128)(2,1)} %bitcast.7, s32[4,16]{1,0:T(4,128)} %bitcast.9), custom_call_target="tpu_custom_call" | custom-call | tf_op jit(solution)/shard_map/pallas_call | solution.py:689
  46.1 3.0 %copy.5 = bf16[512,4,256]{2,1,0:T(4,128)(2,1)} copy(bf16[512,4,256]{2,0,1:T(8,128)(2,1)} %bitcast.6) | data formatting | bytes 2097152 | tf_op jit(solution)/shard_map/transpose | solution.py:715

commit v2 on v1

--- a/solution.py
+++ b/solution.py
@@ -329,24 +329,20 @@
 
 
 def xor_of(index, step):
-    result, weight = 0, 1
-    while weight < 64:
-        bit = lax.rem(index // weight + step // weight, 2)
-        result, weight = result + bit * weight, weight * 2
-    return result
+    return lax.bitwise_xor(jnp.int32(index), jnp.int32(step))
 
 
 def fused_kernel(
     lines, columns, bins, low,
     records_ref, targets_ref, aperture_ref, out_ref,
     records, table, inverse, expand, mixing, apertures, traces_here, traces,
-    sent, spectra, picked_here, picked, running, gathered,
-    load, own, near_send, near_recv, wide_send, wide_recv, run_send, run_recv,
+    sent, spectra, picked_here, picked, running, gathered, raw, stage, result,
+    load, own, near_send, near_recv, wide_send, wide_recv, run_send, run_recv, store,
 ):
     f32, bf16 = jnp.float32, jnp.bfloat16
     devices = lines * columns
     halves = records.shape[0]
-    shots, time_rows, receivers = targets_ref.shape
+    time_rows, shots, receivers = targets_ref.shape
     held = records_ref.shape[0] // receivers
     part = receivers // halves
     gathers = aperture_ref.shape[1]
@@ -383,6 +379,8 @@
             )
     for copy in loads:
         copy.start()
+    raw_load = pltpu.make_async_copy(targets_ref, raw, own.at[7])
+    raw_load.start()
 
     group = 4 * depth // 2
     scale = 1.0 / math.sqrt(NT)
@@ -470,7 +468,17 @@
             device_id_type=mesh_id,
         )
 
+    def unpack_targets():
+        raw_load.wait()
+        rows = time_rows // 4
+        for c in range(4):
+            value = raw[c * rows : (c + 1) * rows].astype(f32)
+            value = value.reshape(rows * shots, receivers)
+            for h in range(halves):
+                stage[h, c * rows * shots : (c + 1) * rows * shots, :] = value[:, h * part : (h + 1) * part]
+
     transform(0)
+    unpack_targets()
     pl.semaphore_wait(barrier, devices - 1)
     for step in range(1, lines):
         along_line(0, step).start()
@@ -499,7 +507,11 @@
     for shot in range(shots):
         hit = (lane % chosen // gathers == shot) & (receiver == wanted)
         onehot = jnp.where(hit, 1.0, 0.0).astype(bf16)
-        total += jnp.dot(targets_ref[shot], onehot, preferred_element_type=f32)
+        for h in range(halves):
+            total += jnp.dot(
+                stage[h, pl.ds(shot, time_rows, stride=shots), :].astype(bf16),
+                onehot[h * part : (h + 1) * part], preferred_element_type=f32,
+            )
     fold = time_rows // 2
     lane = lax.broadcasted_iota(jnp.int32, (fold, lines * width), 1)
     folded = jnp.where(lane % width < chosen, total[:fold], total[fold:]).astype(bf16)
@@ -653,9 +665,28 @@
     def invert(h):
         for shot in range(shots):
             block = gathered[h, :, shot].reshape(2 * NF, part)
-            out_ref[shot, :, h * part : (h + 1) * part] = jnp.dot(
+            stage[h, pl.ds(shot, time_rows, stride=shots), :] = jnp.dot(
                 inverse[...], block, preferred_element_type=f32
-            ).astype(bf16)
+            )
+
+    pieces = 4
+
+    def put(h, c):
+        rows = time_rows // pieces
+        here = (pl.ds(c * rows, rows), slice(None), pl.ds(h * part, part))
+        return pltpu.make_async_copy(result.at[here], out_ref.at[here], store.at[h, c])
+
+    def emit(h):
+        rows = time_rows // pieces
+        lanes = slice(h * part, (h + 1) * part)
+        for c in range(pieces):
+            value = stage[h, c * rows * shots : (c + 1) * rows * shots, :]
+            result[c * rows : (c + 1) * rows, :, lanes] = value.reshape(rows, shots, part).astype(bf16)
+            put(h, c).start()
+
+    def settle(h):
+        for c in range(pieces):
+            put(h, c).wait()
 
     mix(0)
     keep_one.wait()
@@ -666,9 +697,13 @@
     relay(1)
     complete(0)
     invert(0)
+    emit(0)
     turn_over(1)
     complete(1)
     invert(1)
+    emit(1)
+    settle(0)
+    settle(1)
 
 
 def fused(records, targets, aperture):
@@ -684,13 +719,14 @@
     width = 2 * shots * gathers
     wide = held * columns * 2 * bins
     in_vmem = pl.BlockSpec(memory_space=pltpu.VMEM)
+    any_place = pl.BlockSpec(memory_space=pl.ANY)
     dma = pltpu.SemaphoreType.DMA
     vmem = lambda *shape: pltpu.VMEM(shape, bf16)
     out = pl.pallas_call(
         functools.partial(fused_kernel, lines, columns, bins, 10),
-        out_shape=jax.ShapeDtypeStruct((shots, time_rows, receivers), bf16),
-        in_specs=[pl.BlockSpec(memory_space=pl.ANY), in_vmem, in_vmem],
-        out_specs=in_vmem,
+        out_shape=jax.ShapeDtypeStruct((time_rows, shots, receivers), bf16),
+        in_specs=[any_place, any_place, in_vmem],
+        out_specs=any_place,
         scratch_shapes=[
             vmem(halves, held * part, NT),
             vmem(2 * NF, NT),
@@ -706,13 +742,16 @@
             vmem(devices, bins, width),
             vmem(halves, columns, shots, 2 * bins, part),
             vmem(halves, devices, shots, 2 * bins, part),
-            dma((halves, held)), dma((7,)), dma((2, lines)), dma((2, lines)),
+            vmem(time_rows, shots, receivers),
+            pltpu.VMEM((halves, time_rows * shots, part), jnp.float32),
+            vmem(time_rows, shots, receivers),
+            dma((halves, held)), dma((8,)), dma((2, lines)), dma((2, lines)),
             dma((3, devices)), dma((3, devices)),
-            dma((halves, 4, columns)), dma((halves, 4, columns)),
+            dma((halves, 4, columns)), dma((halves, 4, columns)), dma((halves, 4)),
         ],
         compiler_params=pltpu.CompilerParams(collective_id=2, has_side_effects=True),
-    )(records.reshape(held * receivers, NT), targets.transpose(1, 0, 2), aperture.reshape(shots, gathers))
-    return out.transpose(1, 0, 2)
+    )(records.reshape(held * receivers, NT), targets, aperture.reshape(shots, gathers))
+    return out
 
 
 def on_device(records, targets, aperture):

time: 49.4 us -> 46.3 us (0.937)
  local copies, waits for them, and re-layouts: 5.34 us -> 2.56 us
    transpose x1 -> x0, local copies, waits for them, and re-layouts: 3.01 us -> none  [fused(): return out.transpose(1, 0, 2)]
where the time goes in v2:
time: 46.3 us; the launch traced here: 46.1 us
  Pallas kernels  43.6 us (94%)
  local copies, waits for them, and re-layouts  2.56 us (6%)
    pallas_call x1, Pallas kernels, fused(): pl.pallas_call(functools.partial(fused_kernel, lines, columns, bins, 10),...  43.6 us
    unnamed x1, local copies, waits for them, and re-layouts  2.56 us

profile of v2, /device:TPU:0, one launch (start us, length us, event | category | flops | bytes accessed | tf_op | source)
XLA Modules:
  0.0 46.1 jit_solution(9480324085767817098)
XLA Ops:
  0.0 43.6 %shard_map.37 = bf16[512,4,256]{2,1,0:T(4,128)(2,1)} custom-call(bf16[512,2048]{1,0:T(8,128)(2,1)} %bitcast.2, bf16[512,4,256]{2,1,0:T(4,128)(2,1)} %targets_ref.1, s32[4,16]{1,0:T(4,128)} %bitcast.3), custom_call_target="tpu_custom_call" | custom-call | tf_op jit(solution)/shard_map/pallas_call | solution.py:725
  43.6 2.6 %copy.5 = bf16[512,4,256]{2,1,0:T(4,128)(2,1)} copy(bf16[512,4,256]{2,1,0:T(4,128)(2,1)} %shard_map.37) | data formatting | bytes 2097152

commit v3 on v2

--- a/solution.py
+++ b/solution.py
@@ -333,11 +333,11 @@
 
 
 def fused_kernel(
-    lines, columns, bins, low,
+    lines, columns, bins,
     records_ref, targets_ref, aperture_ref, out_ref,
     records, table, inverse, expand, mixing, apertures, traces_here, traces,
-    sent, spectra, picked_here, picked, running, gathered, raw, stage, result,
-    load, own, near_send, near_recv, wide_send, wide_recv, run_send, run_recv, store,
+    sent, spectra, picked_here, picked, running, gathered, raw, stage, unpacked,
+    load, own, near_send, near_recv, wide_send, wide_recv, run_send, across_recv, far_recv, core_recv,
 ):
     f32, bf16 = jnp.float32, jnp.bfloat16
     devices = lines * columns
@@ -381,6 +381,8 @@
         copy.start()
     raw_load = pltpu.make_async_copy(targets_ref, raw, own.at[7])
     raw_load.start()
+    aperture_load = pltpu.make_async_copy(aperture_ref, apertures.at[line], own.at[0])
+    aperture_load.start()
 
     group = 4 * depth // 2
     scale = 1.0 / math.sqrt(NT)
@@ -422,6 +424,17 @@
         )
         sent[h] = value.astype(bf16).reshape(sent.shape[1:])
 
+    def await_all(source, target, count, send_sem, recv_sem):
+        copy = pltpu.make_async_remote_copy(
+            src_ref=source.at[pl.ds(0, count)],
+            dst_ref=target.at[pl.ds(0, count)],
+            send_sem=send_sem,
+            recv_sem=recv_sem,
+            device_id={"xline": xor_of(line, 1)},
+            device_id_type=mesh_id,
+        )
+        copy.wait()
+
     def wide(which, source, target, step):
         far, near = step // 8, lax.rem(step, 8)
         line_step = near // 4 * 2 + lax.rem(near, 2)
@@ -430,8 +443,8 @@
         return pltpu.make_async_remote_copy(
             src_ref=source.at[peer_line * columns + peer_shot],
             dst_ref=target.at[me],
-            send_sem=wide_send.at[which, step],
-            recv_sem=wide_recv.at[which, step],
+            send_sem=wide_send.at[which],
+            recv_sem=wide_recv.at[which],
             device_id={"xline": peer_line, "shot": peer_shot},
             device_id_type=mesh_id,
         )
@@ -441,29 +454,29 @@
             return wide(which, sent.at[which], spectra.at[which], step)
         return wide(which, picked_here, picked, step)
 
-    def start_wide(which, first, last):
+    def start_wide(which, cross):
         def begin(j, _):
-            wide_copy(which, devices - 1 - j).start()
+            wide_copy(which, (3 - j // 4) * 8 + cross * 4 + 3 - lax.rem(j, 4)).start()
             return 0
 
-        lax.fori_loop(first, last, begin, 0)
+        lax.fori_loop(0, devices // 2 - 1 + cross, begin, 0)
 
     def wait_wide(which):
-        def finish(j, _):
-            wide_copy(which, devices - 1 - j).wait()
-            return 0
-
-        lax.fori_loop(0, devices - 1, finish, 0)
+        if which < halves:
+            source, target = sent.at[which], spectra.at[which]
+        else:
+            source, target = picked_here, picked
+        await_all(source, target, devices - 1, wide_send.at[which], wide_recv.at[which])
 
     def along_line(which, step):
         peer = xor_of(line, step)
-        source = traces_here.at[peer] if which else aperture_ref
+        source = traces_here.at[peer] if which else apertures.at[line]
         target = traces if which else apertures
         return pltpu.make_async_remote_copy(
             src_ref=source,
             dst_ref=target.at[line],
-            send_sem=near_send.at[which, step],
-            recv_sem=near_recv.at[which, step],
+            send_sem=near_send.at[which * step],
+            recv_sem=near_recv.at[which * step],
             device_id={"xline": peer},
             device_id_type=mesh_id,
         )
@@ -476,53 +489,15 @@
             value = value.reshape(rows * shots, receivers)
             for h in range(halves):
                 stage[h, c * rows * shots : (c + 1) * rows * shots, :] = value[:, h * part : (h + 1) * part]
+        for shot in range(shots):
+            for h in range(halves):
+                unpacked[shot, :, h * part : (h + 1) * part] = (
+                    stage[h, pl.ds(shot, time_rows, stride=shots), :].astype(bf16)
+                )
 
     transform(0)
     unpack_targets()
-    pl.semaphore_wait(barrier, devices - 1)
-    for step in range(1, lines):
-        along_line(0, step).start()
-    start_wide(0, 0, devices - 1)
-    mine = [
-        pltpu.make_async_copy(aperture_ref, apertures.at[line], own.at[0]),
-        pltpu.make_async_copy(sent.at[0, me], spectra.at[0, me], own.at[1]),
-    ]
-    for copy in mine:
-        copy.start()
     transform(1)
-    keep_one = pltpu.make_async_copy(sent.at[1, me], spectra.at[1, me], own.at[2])
-    keep_one.start()
-    for copy in mine:
-        copy.wait()
-    for step in range(1, lines):
-        along_line(0, step).wait()
-
-    wanted = []
-    for l in range(lines):
-        wanted += [apertures[l, s : s + 1, :] for s in range(shots)] * 2
-    wanted = jnp.concatenate(wanted, axis=1)
-    lane = lax.broadcasted_iota(jnp.int32, (receivers, lines * width), 1)
-    receiver = lax.broadcasted_iota(jnp.int32, (receivers, lines * width), 0)
-    total = jnp.zeros((time_rows, lines * width), f32)
-    for shot in range(shots):
-        hit = (lane % chosen // gathers == shot) & (receiver == wanted)
-        onehot = jnp.where(hit, 1.0, 0.0).astype(bf16)
-        for h in range(halves):
-            total += jnp.dot(
-                stage[h, pl.ds(shot, time_rows, stride=shots), :].astype(bf16),
-                onehot[h * part : (h + 1) * part], preferred_element_type=f32,
-            )
-    fold = time_rows // 2
-    lane = lax.broadcasted_iota(jnp.int32, (fold, lines * width), 1)
-    folded = jnp.where(lane % width < chosen, total[:fold], total[fold:]).astype(bf16)
-    for l in range(lines):
-        traces_here[l] = folded[:, l * width : (l + 1) * width]
-    for step in range(1, lines):
-        along_line(1, step).start()
-    keep = pltpu.make_async_copy(traces_here.at[line], traces.at[line], own.at[3])
-    keep.start()
-    start_wide(1, 0, low)
-
     taken = width
     across = held * columns * depth
     for shot in range(shots):
@@ -542,23 +517,62 @@
         block = table[:, pl.ds(pl.multiple_of(slab + c * 128, 128), 128)].astype(f32)
         inverse[c * 128 : (c + 1) * 128, :] = (block * 2.0).T.astype(bf16)
 
+    aperture_load.wait()
+    pl.semaphore_wait(barrier, devices - 1)
+    for step in range(1, lines):
+        along_line(0, step).start()
+    start_wide(0, 0)
+    start_wide(1, 0)
+    mine = [
+        pltpu.make_async_copy(sent.at[0, me], spectra.at[0, me], own.at[1]),
+    ]
+    for copy in mine:
+        copy.start()
+    keep_one = pltpu.make_async_copy(sent.at[1, me], spectra.at[1, me], own.at[2])
+    keep_one.start()
+    for copy in mine:
+        copy.wait()
+    await_all(apertures, apertures, lines - 1, near_send.at[0], near_recv.at[0])
+
+    fold = time_rows // 2
+    lane = lax.broadcasted_iota(jnp.int32, (fold, width), 1)
+    receiver = lax.broadcasted_iota(jnp.int32, (receivers, width), 0)
+    chosen_by = []
+    for shot in range(shots):
+        wanted = jnp.concatenate([apertures[l, shot : shot + 1, :] for l in range(lines)] * 2, axis=1)
+        onehot = jnp.where(receiver == wanted, 1.0, 0.0).astype(bf16)
+        value = jnp.dot(unpacked[shot], onehot, preferred_element_type=f32)
+        chosen_by.append(jnp.where(lane < chosen, value[:fold], value[fold:]))
+    for l in range(lines):
+        value = chosen_by[l]
+        for shot in range(shots):
+            if shot != l:
+                moved = pltpu.roll(chosen_by[shot], (shot - l) * gathers % width, 1)
+                value = jnp.where(lane // gathers % shots == shot, moved, value)
+        traces_here[l] = value.astype(bf16)
+    for step in (2, 3, 1):
+        along_line(1, step).start()
+    keep = pltpu.make_async_copy(traces_here.at[line], traces.at[line], own.at[3])
+    keep.start()
+    start_wide(0, 1)
+
     keep.wait()
-    for step in range(1, lines):
-        along_line(1, step).wait()
     ahead = jnp.zeros((2 * NF, width), f32)
     behind = jnp.zeros((2 * NF, width), f32)
-    for l in range(lines):
-        base = l * time_rows
-        ahead += jnp.dot(table[:, base : base + fold], traces[l], preferred_element_type=f32)
-        behind += jnp.dot(
-            table[:, base + fold : base + time_rows], traces[l], preferred_element_type=f32
-        )
+    for step in range(lines):
+        l = xor_of(line, step)
+        if step:
+            along_line(1, step).wait()
+        base = pl.multiple_of(l * time_rows, time_rows)
+        ahead += jnp.dot(table[:, pl.ds(base, fold)], traces[l], preferred_element_type=f32)
+        behind += jnp.dot(table[:, pl.ds(base + fold, fold)], traces[l], preferred_element_type=f32)
     real = (ahead + pltpu.roll(behind, chosen, 1)).reshape(devices, depth, width)[:, :bins]
     imag = (pltpu.roll(ahead, chosen, 1) + behind).reshape(devices, depth, width)[:, bins:]
     lane = lax.broadcasted_iota(jnp.int32, (devices, bins, width), 2)
     picked_here[...] = jnp.where(lane < chosen, real, imag).astype(bf16)
-    start_wide(2, 0, devices - 1)
-    start_wide(1, low, devices - 1)
+    start_wide(2, 1)
+    start_wide(2, 0)
+    start_wide(1, 1)
     keep = pltpu.make_async_copy(picked_here.at[me], picked.at[me], own.at[4])
     keep.start()
 
@@ -587,8 +601,8 @@
         return pltpu.make_async_remote_copy(
             src_ref=gathered.at[h, slot],
             dst_ref=gathered.at[h, slot],
-            send_sem=run_send.at[h, stage, step],
-            recv_sem=run_recv.at[h, stage, step],
+            send_sem=run_send.at[h, stage],
+            recv_sem=far_recv.at[h, step] if stage == 2 else core_recv.at[h, stage // 2],
             device_id={"xline": peer_line},
             device_id_type=mesh_id,
         )
@@ -598,8 +612,8 @@
         return pltpu.make_async_remote_copy(
             src_ref=running.at[h, peer],
             dst_ref=gathered.at[h, me],
-            send_sem=run_send.at[h, 0, step],
-            recv_sem=run_recv.at[h, 0, step],
+            send_sem=run_send.at[h, 0],
+            recv_sem=across_recv.at[h, step],
             device_id={"shot": peer},
             device_id_type=mesh_id,
         )
@@ -623,7 +637,7 @@
                 running[h, column, shot] = jnp.concatenate(pieces, axis=0).astype(bf16)
 
         def begin(j, _):
-            spread(h, columns - 1 - j).start()
+            spread(h, lax.select(j == 0, 1, columns - j)).start()
             return 0
 
         lax.fori_loop(0, columns - 1, begin, 0)
@@ -635,8 +649,8 @@
 
     def relay(h):
         def pass_on(j, _):
-            step = j + 1
-            spread(h, step).wait()
+            step = lax.select(j == 0, 1, columns - j)
+            spread(h, step).wait_recv()
             hop(h, 2, line, far_line, step).start()
             hop(h, 1, line, core_line, step).start()
             return 0
@@ -652,15 +666,21 @@
         lax.fori_loop(0, columns, pass_on, 0)
 
     def complete(h):
-        def finish(step, _):
-            hop(h, 1, core_line, core_line, step).wait_recv()
-            hop(h, 3, diagonal_line, core_line, step).wait_recv()
-            hop(h, 1, line, core_line, step).wait_send()
-            hop(h, 2, line, far_line, step).wait_send()
-            hop(h, 3, far_line, core_line, step).wait_send()
-            return 0
-
-        lax.fori_loop(0, columns, finish, 0)
+        def settled(stage, count):
+            source = running.at[h, pl.ds(0, count)]
+            return pltpu.make_async_remote_copy(
+                src_ref=source,
+                dst_ref=gathered.at[h, pl.ds(0, count)],
+                send_sem=run_send.at[h, stage],
+                recv_sem=core_recv.at[h, stage // 2],
+                device_id={"xline": core_line},
+                device_id_type=mesh_id,
+            )
+
+        settled(1, columns).wait()
+        settled(3, columns).wait()
+        settled(2, columns).wait_send()
+        settled(0, columns - 1).wait_send()
 
     def invert(h):
         for shot in range(shots):
@@ -671,22 +691,12 @@
 
     pieces = 4
 
-    def put(h, c):
-        rows = time_rows // pieces
-        here = (pl.ds(c * rows, rows), slice(None), pl.ds(h * part, part))
-        return pltpu.make_async_copy(result.at[here], out_ref.at[here], store.at[h, c])
-
     def emit(h):
         rows = time_rows // pieces
         lanes = slice(h * part, (h + 1) * part)
         for c in range(pieces):
             value = stage[h, c * rows * shots : (c + 1) * rows * shots, :]
-            result[c * rows : (c + 1) * rows, :, lanes] = value.reshape(rows, shots, part).astype(bf16)
-            put(h, c).start()
-
-    def settle(h):
-        for c in range(pieces):
-            put(h, c).wait()
+            out_ref[c * rows : (c + 1) * rows, :, lanes] = value.reshape(rows, shots, part).astype(bf16)
 
     mix(0)
     keep_one.wait()
@@ -702,8 +712,6 @@
     complete(1)
     invert(1)
     emit(1)
-    settle(0)
-    settle(1)
 
 
 def fused(records, targets, aperture):
@@ -718,15 +726,16 @@
     halves, part = 2, receivers // 2
     width = 2 * shots * gathers
     wide = held * columns * 2 * bins
+    stay = lambda array: pltpu.with_memory_space_constraint(array, pltpu.HBM)
     in_vmem = pl.BlockSpec(memory_space=pltpu.VMEM)
-    any_place = pl.BlockSpec(memory_space=pl.ANY)
+    in_hbm = pl.BlockSpec(memory_space=pltpu.HBM)
     dma = pltpu.SemaphoreType.DMA
     vmem = lambda *shape: pltpu.VMEM(shape, bf16)
     out = pl.pallas_call(
-        functools.partial(fused_kernel, lines, columns, bins, 10),
+        functools.partial(fused_kernel, lines, columns, bins),
         out_shape=jax.ShapeDtypeStruct((time_rows, shots, receivers), bf16),
-        in_specs=[any_place, any_place, in_vmem],
-        out_specs=any_place,
+        in_specs=[in_hbm, in_hbm, in_hbm],
+        out_specs=in_vmem,
         scratch_shapes=[
             vmem(halves, held * part, NT),
             vmem(2 * NF, NT),
@@ -744,13 +753,12 @@
             vmem(halves, devices, shots, 2 * bins, part),
             vmem(time_rows, shots, receivers),
             pltpu.VMEM((halves, time_rows * shots, part), jnp.float32),
-            vmem(time_rows, shots, receivers),
-            dma((halves, held)), dma((8,)), dma((2, lines)), dma((2, lines)),
-            dma((3, devices)), dma((3, devices)),
-            dma((halves, 4, columns)), dma((halves, 4, columns)), dma((halves, 4)),
+            vmem(shots, time_rows, receivers),
+            dma((halves, held)), dma((8,)), dma((lines,)), dma((lines,)), dma((3,)), dma((3,)),
+            dma((halves, 4)), dma((halves, columns)), dma((halves, columns)), dma((halves, 2)),
         ],
-        compiler_params=pltpu.CompilerParams(collective_id=2, has_side_effects=True),
-    )(records.reshape(held * receivers, NT), targets, aperture.reshape(shots, gathers))
+        compiler_params=pltpu.CompilerParams(collective_id=2, has_side_effects=True, vmem_limit_bytes=24 << 20),
+    )(stay(records.reshape(held * receivers, NT)), stay(targets), stay(aperture.reshape(shots, gathers)))
     return out
 
 

time: 46.3 us -> 41.6 us (0.90)
  Pallas kernels: 43.6 us -> 40.5 us
  local copies, waits for them, and re-layouts: 2.56 us -> 0.97 us
    pallas_call x1, Pallas kernels: 43.6 us -> 40.5 us  [fused(): pl.pallas_call(functools.partial(fused_kernel, lines, columns, bins), out...]
    unnamed x1, local copies, waits for them, and re-layouts: 2.56 us -> 0.97 us
where the time goes in v3:
time: 41.6 us; the launch traced here: 41.4 us
  Pallas kernels  40.5 us (97%)
  local copies, waits for them, and re-layouts  0.97 us (2%)
    pallas_call x1, Pallas kernels, fused(): pl.pallas_call(functools.partial(fused_kernel, lines, columns, bins), out...  40.5 us
    unnamed x1, local copies, waits for them, and re-layouts  0.97 us

profile of v3, /device:TPU:0, one launch (start us, length us, event | category | flops | bytes accessed | tf_op | source)
XLA Modules:
  0.0 41.4 jit_solution(5316826572642396520)
XLA Ops:
  0.0 40.5 %shard_map.37 = bf16[512,4,256]{2,1,0:T(4,128)(2,1)S(1)} custom-call(bf16[512,2048]{1,0:T(8,128)(2,1)} %bitcast.2, bf16[512,4,256]{2,1,0:T(4,128)(2,1)} %targets_ref.1, s32[4,16]{1,0:T(4,128)} %bitcast.3), custom_call_target="tpu_custom_call" | custom-call | tf_op jit(solution)/shard_map/pallas_call | solution.py:734
  40.5 1.0 %copy.5 = bf16[512,4,256]{2,1,0:T(4,128)(2,1)} copy(bf16[512,4,256]{2,1,0:T(4,128)(2,1)S(1)} %shard_map.37) | data formatting | bytes 2097152

commit v4 on v3

--- a/solution.py
+++ b/solution.py
@@ -356,16 +356,22 @@
     mesh_id = pl.DeviceIdType.MESH
     barrier = pltpu.get_barrier_semaphore()
 
-    def greet(step, _):
-        peer = lax.rem(me + step, devices)
+    def peer_at(step):
+        near = lax.rem(step, 8)
+        line_step = near // 4 * 2 + lax.rem(near, 2)
+        shot_step = step // 8 * 2 + lax.rem(near // 2, 2)
+        return xor_of(line, line_step), xor_of(shot_here, shot_step)
+
+    def greet(j, _):
+        peer_line, peer_shot = peer_at(devices - 1 - j)
         pl.semaphore_signal(
             barrier, inc=1,
-            device_id={"xline": peer // columns, "shot": lax.rem(peer, columns)},
-            device_id_type=mesh_id,
-        )
-        return 0
-
-    lax.fori_loop(1, devices, greet, 0)
+            device_id={"xline": peer_line, "shot": peer_shot},
+            device_id_type=mesh_id,
+        )
+        return 0
+
+    lax.fori_loop(0, devices - 1, greet, 0)
 
     loads = []
     for h in range(halves):
@@ -436,10 +442,7 @@
         copy.wait()
 
     def wide(which, source, target, step):
-        far, near = step // 8, lax.rem(step, 8)
-        line_step = near // 4 * 2 + lax.rem(near, 2)
-        shot_step = far * 2 + lax.rem(near // 2, 2)
-        peer_line, peer_shot = xor_of(line, line_step), xor_of(shot_here, shot_step)
+        peer_line, peer_shot = peer_at(step)
         return pltpu.make_async_remote_copy(
             src_ref=source.at[peer_line * columns + peer_shot],
             dst_ref=target.at[me],
@@ -497,31 +500,12 @@
 
     transform(0)
     unpack_targets()
-    transform(1)
-    taken = width
-    across = held * columns * depth
-    for shot in range(shots):
-        for q in range(2):
-            k = lax.broadcasted_iota(jnp.int32, (taken, held * columns * depth), 0)
-            j = lax.broadcasted_iota(jnp.int32, (taken, held * columns * depth), 1)
-            k_imag, k_shot, k_gather = k // chosen, k // gathers % shots, k % gathers
-            j_held, j_column, j_imag = j // (columns * depth), j // depth % columns, j // bins % 2
-            hit = (k_gather == j_column * held + j_held) & (k_shot == shot)
-            hit = hit & ((k_imag != j_imag) if q else (k_imag == j_imag))
-            value = jnp.where(hit, 1.0, 0.0)
-            if q == 0:
-                value = jnp.where(j_imag == 1, -value, value)
-            expand[shot * 2 + q] = value.astype(bf16)
-    slab = line * time_rows
-    for c in range(time_rows // 128):
-        block = table[:, pl.ds(pl.multiple_of(slab + c * 128, 128), 128)].astype(f32)
-        inverse[c * 128 : (c + 1) * 128, :] = (block * 2.0).T.astype(bf16)
-
     aperture_load.wait()
     pl.semaphore_wait(barrier, devices - 1)
     for step in range(1, lines):
         along_line(0, step).start()
     start_wide(0, 0)
+    transform(1)
     start_wide(1, 0)
     mine = [
         pltpu.make_async_copy(sent.at[0, me], spectra.at[0, me], own.at[1]),
@@ -555,6 +539,25 @@
     keep = pltpu.make_async_copy(traces_here.at[line], traces.at[line], own.at[3])
     keep.start()
     start_wide(0, 1)
+    taken = width
+    across = held * columns * depth
+    for shot in range(shots):
+        for q in range(2):
+            k = lax.broadcasted_iota(jnp.int32, (taken, held * columns * depth), 0)
+            j = lax.broadcasted_iota(jnp.int32, (taken, held * columns * depth), 1)
+            k_imag, k_shot, k_gather = k // chosen, k // gathers % shots, k % gathers
+            j_held, j_column, j_imag = j // (columns * depth), j // depth % columns, j // bins % 2
+            hit = (k_gather == j_column * held + j_held) & (k_shot == shot)
+            hit = hit & ((k_imag != j_imag) if q else (k_imag == j_imag))
+            value = jnp.where(hit, 1.0, 0.0)
+            if q == 0:
+                value = jnp.where(j_imag == 1, -value, value)
+            expand[shot * 2 + q] = value.astype(bf16)
+    slab = line * time_rows
+    for c in range(time_rows // 128):
+        block = table[:, pl.ds(pl.multiple_of(slab + c * 128, 128), 128)].astype(f32)
+        inverse[c * 128 : (c + 1) * 128, :] = (block * 2.0).T.astype(bf16)
+
 
     keep.wait()
     ahead = jnp.zeros((2 * NF, width), f32)
@@ -703,12 +706,12 @@
     wait_wide(1)
     mix(1)
     relay(0)
+    relay(1)
     turn_over(0)
-    relay(1)
+    turn_over(1)
     complete(0)
     invert(0)
     emit(0)
-    turn_over(1)
     complete(1)
     invert(1)
     emit(1)

time: 41.6 us -> 38.1 us (0.916)
  Pallas kernels: 40.5 us -> 36.9 us
    pallas_call x1, Pallas kernels: 40.5 us -> 36.9 us  [fused(): pl.pallas_call(functools.partial(fused_kernel, lines, columns, bins), out...]
where the time goes in v4:
time: 38.1 us; the launch traced here: 37.9 us
  Pallas kernels  36.9 us (97%)
  local copies, waits for them, and re-layouts  0.97 us (3%)
    pallas_call x1, Pallas kernels, fused(): pl.pallas_call(functools.partial(fused_kernel, lines, columns, bins), out...  36.9 us
    unnamed x1, local copies, waits for them, and re-layouts  0.97 us

profile of v4, /device:TPU:0, one launch (start us, length us, event | category | flops | bytes accessed | tf_op | source)
XLA Modules:
  0.0 37.9 jit_solution(13149749464956142496)
XLA Ops:
  0.0 36.9 %shard_map.37 = bf16[512,4,256]{2,1,0:T(4,128)(2,1)S(1)} custom-call(bf16[512,2048]{1,0:T(8,128)(2,1)} %bitcast.2, bf16[512,4,256]{2,1,0:T(4,128)(2,1)} %targets_ref.1, s32[4,16]{1,0:T(4,128)} %bitcast.3), custom_call_target="tpu_custom_call" | custom-call | tf_op jit(solution)/shard_map/pallas_call | solution.py:737
  37.0 1.0 %copy.5 = bf16[512,4,256]{2,1,0:T(4,128)(2,1)} copy(bf16[512,4,256]{2,1,0:T(4,128)(2,1)S(1)} %shard_map.37) | data formatting | bytes 2097152

commit v5 on v4

--- a/solution.py
+++ b/solution.py
@@ -504,9 +504,9 @@
     pl.semaphore_wait(barrier, devices - 1)
     for step in range(1, lines):
         along_line(0, step).start()
+    start_wide(0, 1)
     start_wide(0, 0)
     transform(1)
-    start_wide(1, 0)
     mine = [
         pltpu.make_async_copy(sent.at[0, me], spectra.at[0, me], own.at[1]),
     ]
@@ -538,7 +538,7 @@
         along_line(1, step).start()
     keep = pltpu.make_async_copy(traces_here.at[line], traces.at[line], own.at[3])
     keep.start()
-    start_wide(0, 1)
+    start_wide(1, 0)
     taken = width
     across = held * columns * depth
     for shot in range(shots):
@@ -640,7 +640,7 @@
                 running[h, column, shot] = jnp.concatenate(pieces, axis=0).astype(bf16)
 
         def begin(j, _):
-            spread(h, lax.select(j == 0, 1, columns - j)).start()
+            spread(h, j + 1).start()
             return 0
 
         lax.fori_loop(0, columns - 1, begin, 0)
@@ -652,7 +652,7 @@
 
     def relay(h):
         def pass_on(j, _):
-            step = lax.select(j == 0, 1, columns - j)
+            step = j + 1
             spread(h, step).wait_recv()
             hop(h, 2, line, far_line, step).start()
             hop(h, 1, line, core_line, step).start()
@@ -668,7 +668,7 @@
 
         lax.fori_loop(0, columns, pass_on, 0)
 
-    def complete(h):
+    def complete(h, far):
         def settled(stage, count):
             source = running.at[h, pl.ds(0, count)]
             return pltpu.make_async_remote_copy(
@@ -680,17 +680,24 @@
                 device_id_type=mesh_id,
             )
 
-        settled(1, columns).wait()
-        settled(3, columns).wait()
-        settled(2, columns).wait_send()
-        settled(0, columns - 1).wait_send()
-
-    def invert(h):
+        if far:
+            settled(3, columns).wait()
+            settled(2, columns).wait_send()
+            settled(0, columns - 1).wait_send()
+        else:
+            settled(1, columns).wait()
+
+    def invert(h, far):
+        side = line // 2 + far * (1 - line // 2 * 2)
+        first = pl.multiple_of(side * NF, NF)
+        origin = side * (devices // 2)
         for shot in range(shots):
-            block = gathered[h, :, shot].reshape(2 * NF, part)
-            stage[h, pl.ds(shot, time_rows, stride=shots), :] = jnp.dot(
-                inverse[...], block, preferred_element_type=f32
-            )
+            block = gathered[h, pl.ds(origin, devices // 2), shot].reshape(NF, part)
+            value = jnp.dot(inverse[:, pl.ds(first, NF)], block, preferred_element_type=f32)
+            here = pl.ds(shot, time_rows, stride=shots)
+            if far:
+                value += stage[h, here, :]
+            stage[h, here, :] = value
 
     pieces = 4
 
@@ -708,12 +715,16 @@
     relay(0)
     relay(1)
     turn_over(0)
+    complete(0, 0)
+    invert(0, 0)
     turn_over(1)
-    complete(0)
-    invert(0)
+    complete(1, 0)
+    invert(1, 0)
+    complete(0, 1)
+    invert(0, 1)
     emit(0)
-    complete(1)
-    invert(1)
+    complete(1, 1)
+    invert(1, 1)
     emit(1)
 
 

time: 38.1 us -> 35.7 us (0.937)
  Pallas kernels: 36.9 us -> 34.6 us
    pallas_call x1, Pallas kernels: 36.9 us -> 34.6 us  [fused(): pl.pallas_call(functools.partial(fused_kernel, lines, columns, bins), out...]
where the time goes in v5:
time: 35.7 us; the launch traced here: 35.5 us
  Pallas kernels  34.6 us (97%)
  local copies, waits for them, and re-layouts  0.97 us (3%)
    pallas_call x1, Pallas kernels, fused(): pl.pallas_call(functools.partial(fused_kernel, lines, columns, bins), out...  34.6 us
    unnamed x1, local copies, waits for them, and re-layouts  0.97 us

profile of v5, /device:TPU:0, one launch (start us, length us, event | category | flops | bytes accessed | tf_op | source)
XLA Modules:
  0.0 35.5 jit_solution(17455302158702898415)
XLA Ops:
  0.0 34.6 %shard_map.37 = bf16[512,4,256]{2,1,0:T(4,128)(2,1)S(1)} custom-call(bf16[512,2048]{1,0:T(8,128)(2,1)} %bitcast.2, bf16[512,4,256]{2,1,0:T(4,128)(2,1)} %targets_ref.1, s32[4,16]{1,0:T(4,128)} %bitcast.3), custom_call_target="tpu_custom_call" | custom-call | tf_op jit(solution)/shard_map/pallas_call | solution.py:748
  34.6 1.0 %copy.5 = bf16[512,4,256]{2,1,0:T(4,128)(2,1)} copy(bf16[512,4,256]{2,1,0:T(4,128)(2,1)S(1)} %shard_map.37) | data formatting | bytes 2097152
